TPU v7x, 32 devices: a whole 2x2x4 slice. The times are simulated.
32 devices in a mesh: path: 8 (over z, x), shard: 4 (over y, core).
Axes of the slice: x: 2, y: 2, z: 4, core: 2. Of those that a mesh axis runs over, the one named last changes fastest.
Arguments:
- master: float32 [2, 4096, 2048], P(None, ('path', 'shard')), may hold values from -6 to 6
- momentum: float32 [2, 4096, 2048], P(None, ('path', 'shard')), may hold values from -2 to 2
- routes: int32 [8, 1], replicated, may hold values from 0 to 1
- counts: int32 [8], replicated, may hold values from 1 to 8
- tokens: bfloat16 [12288, 4096], P(('path', 'shard')), may hold values from -6 to 6
- cotangent: bfloat16 [12288, 2048], P(('path', 'shard')), may hold values from -6 to 6
Outputs:
- master_new: float32 [2, 4096, 2048], P(None, ('path', 'shard'))
- momentum_new: float32 [2, 4096, 2048], P(None, ('path', 'shard'))
Inputs may be any that keep to these rules, and one draw needn't show every extreme that they name: `routes`: every module is read by at least one path.
All inputs are finite; a program needn't handle non-finite values.
Results may differ from a plain program's by a relative error of at most 0.0032.
Values may be sent and summed in bfloat16 or wider, within the bound.
No kernel may reach another device: no remote copies, remote signals or barrier semaphores. Data moves between devices by JAX's collectives and lax.ppermute only.
A program may use at most 128 MiB of HBM per device.

v0:
```python
import jax
import jax.numpy as jnp
from jax import lax
from jax.sharding import PartitionSpec as P


def local(master, momentum, routes, counts, tokens, cotangent):
    path_count = routes.shape[0]
    shards = lax.axis_size("shard")
    modules = master.shape[0]
    rows_block = master.shape[1]
    feat_width = master.shape[2]
    tok_rows = tokens.shape[0]
    model_width = tokens.shape[1]
    inv_root = model_width ** (-0.5)
    chosen = routes[:, 0]
    onehot = (chosen[None, :] == jnp.arange(modules, dtype=jnp.int32)[:, None]).astype(jnp.float32)
    outgoing = jnp.take(master.astype(jnp.bfloat16), chosen, axis=0)
    local_rows = lax.all_to_all(outgoing, "path", split_axis=0, concat_axis=0, tiled=True)
    local_weight = local_rows.reshape(path_count * rows_block, feat_width)
    permuted = tokens.reshape(tok_rows, path_count, shards, rows_block)
    permuted = permuted.transpose(0, 2, 1, 3).reshape(tok_rows, model_width)
    columns = lax.all_to_all(permuted, "shard", split_axis=1, concat_axis=0, tiled=True)
    columns_part = permuted
    pre_sum = jnp.dot(
        columns_part,
        lax.all_gather(local_weight, "shard", axis=0, tiled=True),
        preferred_element_type=jnp.float32,
    )
    pre_act = pre_sum * inv_root
    gate_value = jax.nn.sigmoid(pre_act)
    signal = (
        cotangent.astype(jnp.float32) * gate_value * (1.0 + pre_act * (1.0 - gate_value))
    ).astype(jnp.bfloat16)
    columns_part = columns
    product = lax.dot_general(
        columns_part,
        lax.all_gather(signal, "shard", axis=0, tiled=True),
        (((0,), (0,)), ((), ())),
        preferred_element_type=jnp.float32,
    )
    path_grad = (
        (product * inv_root).astype(jnp.bfloat16).reshape(path_count, rows_block, feat_width)
    )
    received = lax.all_to_all(path_grad, "path", split_axis=0, concat_axis=0, tiled=True)
    mixing = onehot * counts.astype(jnp.float32)[None, :]
    mixing = mixing / jnp.sum(mixing, axis=1, keepdims=True)
    flat_recv = received.reshape(path_count, rows_block * feat_width).astype(jnp.float32)
    outer_grad = jnp.dot(mixing, flat_recv, precision=lax.Precision.HIGHEST).reshape(
        modules, rows_block, feat_width
    )
    momentum_new = 0.9 * momentum + outer_grad
    master_new = master - 0.7 * (outer_grad + 0.9 * momentum_new)
    return (master_new, momentum_new)


def solution(mesh):
    placed = (
        P(None, ("path", "shard"), None),
        P(None, ("path", "shard"), None),
        P(),
        P(),
        P(("path", "shard"), None),
        P(("path", "shard"), None),
    )
    return jax.shard_map(
        local,
        mesh=mesh,
        in_specs=placed,
        out_specs=(P(None, ("path", "shard"), None), P(None, ("path", "shard"), None)),
        check_vma=False,
    )
```

profile of v0, /device:TPU:0, one launch (start us, length us, event | category | flops | bytes accessed | tf_op | source)
XLA Modules:
  0.0 444.9 jit_solution(9973681836863088704)
XLA Ops:
  7.2 0.0 all-gather.3.cloned.1.call-start
  7.2 0.7 fusion.16
  7.9 0.7 and_bitcast_fusion
  8.5 1.7 convert_element_type.22
  10.3 2.8 gather_fusion
  13.0 2.7 broadcast_select_fusion
  15.7 100.3 %all_to_all.29 = bf16[8,128,2048]{2,1,0:T(8,128)(2,1)} all-to-all(bf16[8,128,2048]{2,1,0:T(8,128)(2,1)S(1)} %broadcast_select_fusion), channel_id=1, replica_groups=mesh['path'=8,'shard'=4] {'path'}, dimensions={0} | all-to-all | bytes 8388608 | tf_op jit(solution)/shard_map/all_to_all | solution.py:19
  116.0 0.0 copy-start
  116.0 0.0 all-gather.3.cloned.1.call-update
  116.1 0.0 all-gather.5.cloned.1.call-start
  116.1 1.8 copy-done
  117.9 2.8 copy.27
  120.7 2.7 copy.28
  123.5 2.8 copy.26
  126.3 94.9 %all-gather.3.cloned.1.call-done = bf16[4096,2048]{1,0:T(8,128)(2,1)} async-done(((bf16[1024,2048]{1,0:T(8,128)(2,1)}), bf16[4096,2048]{1,0:T(8,128)(2,1)}) %all-gather.3.cloned.1.call-update) | async-done | bytes 16777232 | tf_op jit(solution)/shard_map/all_gather | solution.py:27
  221.2 14.3 %fusion.5 = bf16[384,2048]{0,1:T(8,128)(2,1)} fusion(bf16[384,2048]{0,1:T(8,128)(2,1)} %copy.26, bf16[4096,2048]{1,0:T(8,128)(2,1)} %all-gather.3.cloned.1.call-done, bf16[384,4096]{0,1:T(8,128)(2,1)S(1)} %bitcast.51), kind=kOutput, calls=%fused_computation.11 | convolution fusion | flops 6451101696 | bytes 23068672 | tf_op jit(solution)/shard_map/dot_general | solution.py:25
  235.5 0.0 all-gather.5.cloned.1.call-update
  235.5 69.7 %all_to_all.30 = bf16[384,4,1024]{0,2,1:T(8,128)(2,1)} all-to-all(bf16[384,4,1024]{0,2,1:T(8,128)(2,1)S(1)} %bitcast.52), channel_id=1, replica_groups=mesh['path'=8,'shard'=4] {'shard'}, dimensions={1} | all-to-all | bytes 6291456 | tf_op jit(solution)/shard_map/all_to_all | solution.py:23
  305.1 3.2 copy.30
  308.4 2.6 all-gather.5.cloned.1.call-done
  311.0 11.1 %multiply_convert_fusion = bf16[2048,1024]{0,1:T(8,128)(2,1)} fusion(bf16[1536,2048]{0,1:T(8,128)(2,1)} %all-gather.5.cloned.1.call-done, bf16[1536,1024]{1,0:T(8,128)(2,1)S(1)} %bitcast.56), kind=kOutput, calls=%fused_computation.1 | convolution fusion | flops 6446645248 | bytes 13631488 | tf_op jit(solution)/shard_map/dot_general | solution.py:36
  322.1 0.0 copy-start.2
  322.1 0.0 copy-start.3
  322.1 5.6 %all-to-all-start.2 = ((bf16[8,128,2048]{2,1,0:T(8,128)(2,1)}), bf16[8,128,2048]{2,1,0:T(8,128)(2,1)}, u32[]{:S(2)}, u32[]{:S(2)}) async-start(bf16[8,128,2048]{2,1,0:T(8,128)(2,1)} %bitcast.55), calls=%async_computation.2 | async-start | bytes 8388608 | tf_op jit(solution)/shard_map/all_to_all | solution.py:45
  327.8 0.0 copy-done.2
  327.8 0.0 copy-done.3
  327.8 0.1 fusion.10
  327.9 93.6 %all-to-all-done.2 = bf16[8,128,2048]{2,1,0:T(8,128)(2,1)} async-done(((bf16[8,128,2048]{2,1,0:T(8,128)(2,1)}), bf16[8,128,2048]{2,1,0:T(8,128)(2,1)}, u32[]{:S(2)}, u32[]{:S(2)}) %all-to-all-start.2) | async-done | bytes 4194336 | tf_op jit(solution)/shard_map/all_to_all | solution.py:45
  421.5 0.0 copy-done.1
  421.5 11.5 %fusion.6 = (f32[2,128,2048]{2,0,1:T(2,128)S(1)}, f32[2,128,2048]{2,0,1:T(2,128)S(1)}) fusion(f32[2,128,2048]{2,1,0:T(8,128)} %param.7, f32[2,128,2048]{2,1,0:T(8,128)S(1)} %copy-done.1, f32[2]{0:T(128)S(1)} %fusion.10, f32[8]{0:T(128)S(1)} %convert_element_type.20, s32[8]{0:T(128)S(1)} %bitcast.58, bf16[1,8,128,2048]{3,2,1,0:T(8,128)(2,1)} %bitcast.19), kind=kOutput, calls=%fused_computation.14 | convolution fusion | flops 53477424 | bytes 12582984 | tf_op jit(solution)/shard_map/dot_general | solution.py:49
  433.0 2.5 copy.33
  435.5 2.5 copy.34
  (3 shorter events, 0.0 us)
Async XLA Ops:
  7.2 214.0 %all-gather.3.cloned.1.call-start = ((), (), s32[]{:S(2)}) async-start(), calls=%async_computation.3 | async-start | bytes 20971520 | tf_op jit(solution)/shard_map/all_gather | solution.py:27
  116.0 1.9 copy-start
  116.1 194.9 %all-gather.5.cloned.1.call-start = ((), (), s32[]{:S(2)}) async-start(), calls=%async_computation.4 | async-start | bytes 7864320 | tf_op jit(solution)/shard_map/all_gather | solution.py:38
  322.1 5.7 %copy-start.2 = (s32[8]{0:T(128)S(1)}, s32[8]{0:T(128)}, u32[]{:S(2)}) copy-start(s32[8]{0:T(128)} %param.9) | copy-start | bytes 100
  322.1 5.7 %copy-start.3 = (s32[8,1]{0,1:T(1,128)S(1)}, s32[8,1]{0,1:T(1,128)}, u32[]{:S(2)}) copy-start(s32[8,1]{0,1:T(1,128)} %param.8) | copy-start | bytes 100
  322.1 99.3 %copy-start.1 = (f32[2,128,2048]{2,1,0:T(8,128)S(1)}, f32[2,128,2048]{2,1,0:T(8,128)}, u32[]{:S(2)}) copy-start(f32[2,128,2048]{2,1,0:T(8,128)} %param.6) | copy-start | bytes 6291460
  322.1 99.3 %all-to-all-start.2 = ((bf16[8,128,2048]{2,1,0:T(8,128)(2,1)}), bf16[8,128,2048]{2,1,0:T(8,128)(2,1)}, u32[]{:S(2)}, u32[]{:S(2)}) async-start(bf16[8,128,2048]{2,1,0:T(8,128)(2,1)} %bitcast.55), calls=%async_computation.2 | async-start | bytes 8388608 | tf_op jit(solution)/shard_map/all_to_all | solution.py:45
Sparse Core Ops, SparseCore 0:
  116.2 104.9 all-gather.2
  235.6 75.3 all-gather.4
where the time goes:
time: 445 us
  waiting for transfers between devices  191 us (43%)
  blocking collectives  170 us (38%)
  matrix products  36.9 us (8%)
  local copies, waits for them, and re-layouts  21.2 us (5%)
  between operations  14.1 us (3%)
  other arithmetic  5.83 us (1%)
  starting transfers between devices  5.72 us (1%)
    all_to_all x1, blocking collectives, local(): lax.all_to_all(outgoing, 'path', split_axis=0, concat_axis=0, tiled=True)  100 us
    all_gather x1, waiting for transfers between devices, local(): lax.all_gather(local_weight, 'shard', axis=0, tiled=True)  94.9 us
    all_to_all x1, waiting for transfers between devices, local(): lax.all_to_all(path_grad, 'path', split_axis=0, concat_axis=0, tiled=True)  93.6 us
    all_to_all x1, blocking collectives, local(): lax.all_to_all(permuted, 'shard', split_axis=1, concat_axis=0, tiled=True)  69.7 us
    dot_general x1, matrix products, local(): jnp.dot(columns_part, lax.all_gather(local_weight, 'shard', axis=0, tiled...  14.3 us
    unnamed x12, local copies, waits for them, and re-layouts  12.5 us
    dot_general x1, matrix products, local(): jnp.dot(mixing, flat_recv, precision=lax.Precision.HIGHEST)  11.5 us
    dot_general x1, matrix products, local(): lax.dot_general(columns_part, lax.all_gather(signal, 'shard', axis=0, til...  11.1 us
  transfers between devices with their start and end apart: 3, of which 3 were waited for; matrix products, arithmetic and copies ran while one was open for 3% of the time, Pallas kernels for 0%

commit v1 on v0

--- a/solution.py
+++ b/solution.py
@@ -2,6 +2,19 @@
 import jax.numpy as jnp
 from jax import lax
 from jax.sharding import PartitionSpec as P
+
+
+def ring_gather(value, axis, dim):
+    ways = lax.axis_size(axis)
+    up = [(d, (d + 1) % ways) for d in range(ways)]
+    down = [(d, (d - 1) % ways) for d in range(ways)]
+    earlier, later = ([value], [value])
+    for _ in range(ways // 2):
+        earlier.append(lax.ppermute(earlier[-1], axis, up))
+    for _ in range((ways - 1) // 2):
+        later.append(lax.ppermute(later[-1], axis, down))
+    line = jnp.concatenate([*earlier[::-1], *later[1:]], axis=dim)
+    return jnp.roll(line, (lax.axis_index(axis) - ways // 2) * value.shape[dim], axis=dim)
 
 
 def local(master, momentum, routes, counts, tokens, cotangent):
@@ -23,9 +36,7 @@
     columns = lax.all_to_all(permuted, "shard", split_axis=1, concat_axis=0, tiled=True)
     columns_part = permuted
     pre_sum = jnp.dot(
-        columns_part,
-        lax.all_gather(local_weight, "shard", axis=0, tiled=True),
-        preferred_element_type=jnp.float32,
+        columns_part, ring_gather(local_weight, "shard", 0), preferred_element_type=jnp.float32
     )
     pre_act = pre_sum * inv_root
     gate_value = jax.nn.sigmoid(pre_act)

time: 445 us -> 518 us (1.16)
  local copies, waits for them, and re-layouts: 21.2 us -> 56.6 us
  waiting for transfers between devices: 191 us -> 226 us
    ppermute x0 -> x3, waiting for transfers between devices: none -> 130 us  [the longest x2 130 us: ring_gather(): earlier.append(lax.ppermute(earlier[-1], axis, up))]
    all_gather x1 -> x0, waiting for transfers between devices: 94.9 us -> none  [local(): lax.all_gather(local_weight, 'shard', axis=0, tiled=True)]
    unnamed x12 -> x21, local copies, waits for them, and re-layouts: 12.5 us -> 43.6 us
  transfers between devices with their start and end apart: 3 -> 5, of which waited for: 3 -> 4; matrix products, arithmetic and copies ran while one was open for 3% -> 5% of each run, Pallas kernels for 0% -> 0%
where the time goes in v1:
time: 518 us; the launch traced here: 517 us
  waiting for transfers between devices  226 us (44%)
  blocking collectives  172 us (33%)
  local copies, waits for them, and re-layouts  56.6 us (11%)
  matrix products  36.8 us (7%)
  between operations  14.1 us (3%)
  starting transfers between devices  6.46 us (1%)
  other arithmetic  5.83 us (1%)
    ppermute x2, waiting for transfers between devices, ring_gather(): earlier.append(lax.ppermute(earlier[-1], axis, up))  130 us
    all_to_all x1, blocking collectives, local(): lax.all_to_all(outgoing, 'path', split_axis=0, concat_axis=0, tiled=True)  101 us
    all_to_all x1, waiting for transfers between devices, local(): lax.all_to_all(path_grad, 'path', split_axis=0, concat_axis=0, tiled=True)  93.7 us
    all_to_all x1, blocking collectives, local(): lax.all_to_all(permuted, 'shard', split_axis=1, concat_axis=0, tiled=True)  70.9 us
    unnamed x21, local copies, waits for them, and re-layouts  43.6 us
    dot_general x1, matrix products, local(): jnp.dot(columns_part, ring_gather(local_weight, 'shard', 0), preferred_el...  14.1 us
    dot_general x1, matrix products, local(): jnp.dot(mixing, flat_recv, precision=lax.Precision.HIGHEST)  11.5 us
    dot_general x1, matrix products, local(): lax.dot_general(columns_part, lax.all_gather(signal, 'shard', axis=0, til...  11.2 us
  transfers between devices with their start and end apart: 5, of which 4 were waited for; matrix products, arithmetic and copies ran while one was open for 5% of the time, Pallas kernels for 0%

profile of v1, /device:TPU:0, one launch (start us, length us, event | category | flops | bytes accessed | tf_op | source)
XLA Modules:
  0.0 517.0 jit_solution(8054999074292243938)
XLA Ops:
  7.2 0.0 all-gather.2.cloned.1.call-start
  7.2 0.7 fusion.24
  7.9 0.7 and_bitcast_fusion
  8.5 1.7 convert_element_type.22
  10.3 2.8 gather_fusion
  13.1 2.7 broadcast_select_fusion
  15.7 100.6 %all_to_all.29 = bf16[8,128,2048]{2,1,0:T(8,128)(2,1)} all-to-all(bf16[8,128,2048]{2,1,0:T(8,128)(2,1)S(1)} %broadcast_select_fusion), channel_id=1, replica_groups=mesh['path'=8,'shard'=4] {'path'}, dimensions={0} | all-to-all | bytes 8388608 | tf_op jit(solution)/shard_map/all_to_all | solution.py:32
  116.3 48.2 %collective-permute-done = bf16[1024,2048]{1,0:T(8,128)(2,1)} collective-permute-done((bf16[1024,2048]{1,0:T(8,128)(2,1)}, bf16[1024,2048]{1,0:T(8,128)(2,1)}, u32[]{:S(2)}, u32[]{:S(2)}) %collective-permute-start) | collective-permute-done | bytes 4194336 | tf_op jit(solution)/shard_map/ppermute | solution.py:13
  164.6 1.7 collective-permute-start.2
  166.3 2.8 copy.27
  169.1 2.2 copy.28
  171.4 2.6 copy.26
  173.9 81.9 %collective-permute-done.1 = bf16[1024,2048]{1,0:T(8,128)(2,1)} collective-permute-done((bf16[1024,2048]{1,0:T(8,128)(2,1)}, bf16[1024,2048]{1,0:T(8,128)(2,1)}, u32[]{:S(2)}, u32[]{:S(2)}) %collective-permute-start.1) | collective-permute-done | bytes 4194336 | tf_op jit(solution)/shard_map/ppermute | solution.py:13
  255.9 4.7 constant_dynamic-update-slice_fusion.7
  260.6 4.7 constant_dynamic-update-slice_fusion.6
  265.3 4.7 constant_dynamic-update-slice_fusion.5
  270.1 4.7 constant_dynamic-update-slice_fusion.4
  274.8 4.7 constant_dynamic-update-slice_fusion.3
  279.5 4.7 constant_dynamic-update-slice_fusion.2
  284.2 4.7 constant_dynamic-update-slice_fusion.1
  289.0 4.8 constant_dynamic-update-slice_fusion
  293.8 14.1 %fusion.10 = bf16[384,2048]{0,1:T(8,128)(2,1)} fusion(bf16[384,2048]{0,1:T(8,128)(2,1)S(1)} %copy-done.2, bf16[384,4096]{0,1:T(8,128)(2,1)S(1)} %bitcast.49, bf16[8192,2048]{1,0:T(8,128)(2,1)} %constant_dynamic-update-slice_fusion, s32[]{:T(128)S(6)} %select_n.27), kind=kOutput, calls=%fused_computation.13 | convolution fusion | flops 6451101696 | bytes 23068676 | tf_op jit(solution)/shard_map/dot_general | solution.py:38
  308.0 70.9 %all_to_all.30 = bf16[384,4,1024]{0,2,1:T(8,128)(2,1)} all-to-all(bf16[384,4,1024]{0,2,1:T(8,128)(2,1)S(1)} %bitcast.50), channel_id=1, replica_groups=mesh['path'=8,'shard'=4] {'shard'}, dimensions={1} | all-to-all | bytes 6291456 | tf_op jit(solution)/shard_map/all_to_all | solution.py:36
  378.9 3.2 copy.30
  382.1 1.9 all-gather.2.cloned.1.call-done
  383.9 11.2 %multiply_convert_fusion = bf16[2048,1024]{0,1:T(8,128)(2,1)} fusion(bf16[1536,2048]{0,1:T(8,128)(2,1)} %all-gather.2.cloned.1.call-done, bf16[1536,1024]{1,0:T(8,128)(2,1)S(1)} %bitcast.54), kind=kOutput, calls=%fused_computation.3 | convolution fusion | flops 6446645248 | bytes 13631488 | tf_op jit(solution)/shard_map/dot_general | solution.py:47
  395.1 4.7 all-to-all-start.2
  399.8 0.1 fusion.17
  399.9 93.7 %all-to-all-done.2 = bf16[8,128,2048]{2,1,0:T(8,128)(2,1)} async-done(((bf16[8,128,2048]{2,1,0:T(8,128)(2,1)}), bf16[8,128,2048]{2,1,0:T(8,128)(2,1)}, u32[]{:S(2)}, u32[]{:S(2)}) %all-to-all-start.2) | async-done | bytes 4194336 | tf_op jit(solution)/shard_map/all_to_all | solution.py:56
  493.6 11.5 %fusion.13 = (f32[2,128,2048]{2,0,1:T(2,128)S(1)}, f32[2,128,2048]{2,0,1:T(2,128)S(1)}) fusion(f32[2,128,2048]{2,1,0:T(8,128)} %param.7, f32[2,128,2048]{2,1,0:T(8,128)S(1)} %copy-done.1, f32[2]{0:T(128)S(1)} %fusion.17, f32[8]{0:T(128)S(1)} %convert_element_type.20, s32[8]{0:T(128)S(1)} %bitcast.56, bf16[1,8,128,2048]{3,2,1,0:T(8,128)(2,1)} %bitcast.19), kind=kOutput, calls=%fused_computation.16 | convolution fusion | flops 53477424 | bytes 12582984 | tf_op jit(solution)/shard_map/dot_general | solution.py:60
  505.1 2.5 copy.33
  507.7 2.5 copy.34
  (16 shorter events, 0.1 us)
Async XLA Ops:
  7.2 376.8 %all-gather.2.cloned.1.call-start = ((), (), s32[]{:S(2)}) async-start(), calls=%async_computation.3 | async-start | bytes 7864320 | tf_op jit(solution)/shard_map/all_gather | solution.py:49
  15.7 150.6 %copy-start = (bf16[384,4096]{1,0:T(8,128)(2,1)S(1)}, bf16[384,4096]{1,0:T(8,128)(2,1)}, u32[]{:S(2)}) copy-start(bf16[384,4096]{1,0:T(8,128)(2,1)} %param.10) | copy-start | bytes 9437188
  116.3 48.2 %collective-permute-start = (bf16[1024,2048]{1,0:T(8,128)(2,1)}, bf16[1024,2048]{1,0:T(8,128)(2,1)}, u32[]{:S(2)}, u32[]{:S(2)}) collective-permute-start(bf16[1024,2048]{1,0:T(8,128)(2,1)} %bitcast.4), channel_id=1, source_target_pairs={{0,1},{1,2},{2,3},{3,0},{4,5},{5,6},{6,7},{7,4},{8,9},{9,10},{10,1... | collective-permute-start | bytes 12582920 | tf_op jit(solution)/shard_map/ppermute | solution.py:13
  164.6 91.3 %collective-permute-start.1 = (bf16[1024,2048]{1,0:T(8,128)(2,1)}, bf16[1024,2048]{1,0:T(8,128)(2,1)}, u32[]{:S(2)}, u32[]{:S(2)}) collective-permute-start(bf16[1024,2048]{1,0:T(8,128)(2,1)} %collective-permute-done), channel_id=1, source_target_pairs={{0,1},{1,2},{2,3},{3,0},{4,5},{5,6},{6,7},{7,4},{8,9},{9,10},{10,1... | collective-permute-start | bytes 12582920 | tf_op jit(solution)/shard_map/ppermute | solution.py:13
  164.6 105.5 %collective-permute-start.2 = (bf16[1024,2048]{1,0:T(8,128)(2,1)}, bf16[1024,2048]{1,0:T(8,128)(2,1)}, u32[]{:S(2)}, u32[]{:S(2)}) collective-permute-start(bf16[1024,2048]{1,0:T(8,128)(2,1)} %bitcast.4), channel_id=1, source_target_pairs={{0,3},{1,0},{2,1},{3,2},{4,7},{5,4},{6,5},{7,6},{8,11},{9,8},{10,9... | collective-permute-start | bytes 12582920 | tf_op jit(solution)/shard_map/ppermute | solution.py:15
  289.0 4.8 copy-start.2
  395.1 4.7 copy-start.3
  395.1 4.7 copy-start.4
  395.1 98.6 %copy-start.1 = (f32[2,128,2048]{2,1,0:T(8,128)S(1)}, f32[2,128,2048]{2,1,0:T(8,128)}, u32[]{:S(2)}) copy-start(f32[2,128,2048]{2,1,0:T(8,128)} %param.6) | copy-start | bytes 6291460
  395.1 98.5 %all-to-all-start.2 = ((bf16[8,128,2048]{2,1,0:T(8,128)(2,1)}), bf16[8,128,2048]{2,1,0:T(8,128)(2,1)}, u32[]{:S(2)}, u32[]{:S(2)}) async-start(bf16[8,128,2048]{2,1,0:T(8,128)(2,1)} %bitcast.53), calls=%async_computation.2 | async-start | bytes 8388608 | tf_op jit(solution)/shard_map/all_to_all | solution.py:56
Sparse Core Ops, SparseCore 0:
  308.1 75.7 all-gather.1
